TPU v7x, 512 devices: a whole 4x8x8 slice. The times are simulated.
512 devices in a mesh: tensor: 8 (over z_hi, core), ctx: 64 (over x, z_lo, y).
Axes of the slice: x: 4, y: 8, z: 8 (z_hi: 4, z_lo: 2; z = z_hi * 2 + z_lo), core: 2. Of those that a mesh axis runs over, the one named last changes fastest.
Arguments:
- queries: bfloat16 [1024, 3072], P('ctx', 'tensor'), may hold values from -12 to 12
- key_cache: bfloat16 [128, 512, 3072], P('ctx', None, 'tensor'), may hold values from -12 to 12
- value_cache: bfloat16 [128, 512, 3072], P('ctx', None, 'tensor'), may hold values from -6 to 6
- cached_len: int32 [4], replicated, may hold values from 3968 to 7936, as said below
- block_slot: int32 [4, 16], replicated, may hold values from -1 to 127, as said below
- out_weight: bfloat16 [3072, 3072], P('tensor', 'ctx'), may hold values from -3 to 3
- norm_gain: float32 [3072], P('tensor'), may hold values from 0.5 to 1.5
Outputs:
- normed: bfloat16 [1024, 3072], P('ctx', 'tensor')
Inputs may be any that keep to these rules, and one draw needn't show every extreme that they name: `cached_len`: one request has exactly 7936 cached tokens. `block_slot`: entry [r, b] is a slot number (device index along ctx times 2 plus the slot on that device) for b below ceil((cached_len[r] + 256) / 512), and -1 beyond; no slot is named twice; the 2 slots of some device are all named.
All inputs are finite; a program needn't handle non-finite values.
Results may differ from a plain program's by a relative error of at most 0.018.
Values may be sent and summed in bfloat16 or wider, within the bound.
A program may use at most 64 MiB of HBM per device.

v0:
```python
import math

import jax
import jax.numpy as jnp
from jax import lax
from jax.sharding import PartitionSpec as P

HD = 96
REQS = 4


masked_score = -1e30


def slot_layout(block_slot, slots):
    slot_ids = lax.axis_index("ctx") * slots + jnp.arange(slots, dtype=jnp.int32)
    matches = block_slot[None, :, :] == slot_ids[:, None, None]
    requests = jnp.arange(block_slot.shape[0], dtype=jnp.int32)[None, :, None]
    entries = jnp.arange(block_slot.shape[1], dtype=jnp.int32)[None, None, :]
    req_of = jnp.sum(jnp.where(matches, requests, 0), axis=(1, 2))
    blk_of = jnp.sum(jnp.where(matches, entries, 0), axis=(1, 2))
    used = jnp.any(matches, axis=(1, 2))
    in_use = jnp.sum(used.astype(jnp.int32))
    visit = jnp.argsort(jnp.where(used, 0, slots) + jnp.arange(slots, dtype=jnp.int32))
    return (req_of, blk_of, in_use, visit)


def block_scores(gathered, key_cache, cached_len, request, first_key, slot):
    block_rows, features = (key_cache.shape[1], key_cache.shape[2])
    heads_dev = features // HD
    span_rows = gathered.shape[0] // REQS
    query_rows = lax.dynamic_slice_in_dim(gathered, request * span_rows, span_rows, 0)
    query_rows = query_rows.reshape(span_rows, heads_dev, HD)
    key_rows = lax.dynamic_index_in_dim(key_cache, slot, 0, keepdims=False).reshape(
        block_rows, heads_dev, HD
    )
    scores = jnp.einsum("qhd,khd->hqk", query_rows, key_rows, preferred_element_type=jnp.float32)
    scores = scores * (1.0 / math.sqrt(HD))
    query_pos = cached_len[request] + jnp.arange(span_rows, dtype=jnp.int32)
    key_pos = first_key + jnp.arange(block_rows, dtype=jnp.int32)
    visible = (key_pos[None, :] <= query_pos[:, None])[None, :, :]
    return (scores, visible)


def body(queries, key_cache, value_cache, cached_len, block_slot, out_weight, norm_gain):
    slots, block_rows, features = key_cache.shape
    heads_dev = features // HD
    own_rows = queries.shape[0]
    n_ctx = lax.axis_size("ctx")
    gathered = lax.all_gather(queries, "ctx", axis=0, tiled=True)
    total_rows = gathered.shape[0]
    span_rows = total_rows // REQS
    req_of, blk_of, in_use, visit = slot_layout(block_slot, slots)

    def weighted(weights, slot):
        value_rows = lax.dynamic_index_in_dim(value_cache, slot, 0, keepdims=False)
        value_rows = value_rows.reshape(block_rows, heads_dev, HD)
        return jnp.einsum(
            "hqk,khd->qhd",
            weights.astype(jnp.bfloat16),
            value_rows,
            preferred_element_type=jnp.float32,
        )

    def scores_of(step):
        slot = visit[step]
        request = req_of[slot]
        scores, visible = block_scores(
            gathered, key_cache, cached_len, request, blk_of[slot] * block_rows, slot
        )
        return (slot, request * span_rows, scores, visible)

    empty_out = jnp.zeros((total_rows, features), jnp.float32)
    empty_mass = jnp.zeros((total_rows, heads_dev), jnp.float32)
    empty_top = jnp.full((total_rows, heads_dev), masked_score, jnp.float32)

    def add_block(step, running):
        out_sum, top_acc, mass_acc = running
        slot, begin, scores, visible = scores_of(step)
        block_top = jnp.max(jnp.where(visible, scores, masked_score), axis=2)
        weights = jnp.where(visible, jnp.exp(scores - block_top[:, :, None]), 0.0)
        block_mass = jnp.sum(weights, axis=2).T
        block_out = weighted(weights, slot)
        old_out = lax.dynamic_slice_in_dim(out_sum, begin, span_rows, 0).reshape(
            span_rows, heads_dev, HD
        )
        old_top = lax.dynamic_slice_in_dim(top_acc, begin, span_rows, 0)
        old_mass = lax.dynamic_slice_in_dim(mass_acc, begin, span_rows, 0)
        new_top = jnp.maximum(old_top, block_top.T)
        keep = jnp.exp(old_top - new_top)
        take = jnp.exp(block_top.T - new_top)
        merged = old_out * keep[:, :, None] + block_out * take[:, :, None]
        out_sum = lax.dynamic_update_slice_in_dim(
            out_sum, merged.reshape(span_rows, features), begin, 0
        )
        top_acc = lax.dynamic_update_slice_in_dim(top_acc, new_top, begin, 0)
        mass_acc = lax.dynamic_update_slice_in_dim(
            mass_acc, old_mass * keep + block_mass * take, begin, 0
        )
        return (out_sum, top_acc, mass_acc)

    out_sum, top_acc, mass_acc = lax.fori_loop(
        0, in_use, add_block, (empty_out, empty_top, empty_mass)
    )
    outs = lax.all_to_all(
        out_sum.reshape(n_ctx, own_rows, features), "ctx", split_axis=0, concat_axis=0, tiled=True
    )
    tops = lax.all_to_all(
        top_acc.reshape(n_ctx, own_rows, heads_dev), "ctx", split_axis=0, concat_axis=0, tiled=True
    )
    masses = lax.all_to_all(
        mass_acc.reshape(n_ctx, own_rows, heads_dev), "ctx", split_axis=0, concat_axis=0, tiled=True
    )
    sources = outs.shape[0]
    items = outs.shape[1]
    best = jnp.max(tops, axis=0)
    factor = jnp.exp(tops - best[None, :, :])
    totals = jnp.sum(masses * factor, axis=0)
    merged = jnp.sum(outs.reshape(sources, items, heads_dev, HD) * factor[:, :, :, None], axis=0)
    attn_full = (merged / totals[:, :, None]).reshape(items, features)
    attn = attn_full.astype(jnp.bfloat16)
    proj = jnp.dot(
        attn,
        lax.all_gather(out_weight, "ctx", axis=1, tiled=True),
        preferred_element_type=jnp.float32,
    )
    share_cols = norm_gain.shape[0]
    summed_rows = lax.psum(proj.astype(jnp.bfloat16), "tensor").astype(jnp.float32)
    mean_square = jnp.mean(summed_rows * summed_rows, axis=1, keepdims=True)
    own_cols = lax.dynamic_slice_in_dim(
        summed_rows, lax.axis_index("tensor") * share_cols, share_cols, 1
    )
    return (own_cols * lax.rsqrt(mean_square + 1e-05) * norm_gain[None, :]).astype(jnp.bfloat16)


def solution(mesh):
    in_specs = (
        P("ctx", "tensor"),
        P("ctx", None, "tensor"),
        P("ctx", None, "tensor"),
        P(),
        P(),
        P("tensor", "ctx"),
        P("tensor"),
    )
    out_specs = P("ctx", "tensor")
    return jax.shard_map(body, mesh=mesh, in_specs=in_specs, out_specs=out_specs, check_vma=False)
```

profile of v0, /device:TPU:1, one launch (start us, length us, event | category | flops | bytes accessed | tf_op | source)
XLA Modules:
  0.0 406.7 jit_solution(11934550049143040198)
XLA Ops:
  6.5 0.0 copy-start.1
  6.5 0.0 all-gather.2.cloned.1.call-start
  6.5 0.7 all-gather.2.cloned.1.call-update
  7.3 0.9 compare_reduce_fusion
  8.1 0.9 fusion.15
  9.1 0.7 iota_add_fusion.2
  9.7 146.6 %all_gather.6 = bf16[1024,384]{1,0:T(8,128)(2,1)} all-gather(bf16[16,384]{1,0:T(8,128)(2,1)} %param.9), channel_id=1, replica_groups=mesh['tensor'=8,'ctx'=64] {'ctx'}, dimensions={0}, use_global_device_ids=true | all-gather | bytes 798720 | tf_op jit(solution)/shard_map/all_gather | solution.py:50
  156.3 0.6 sort.17
  156.9 1.3 broadcast_in_dim.72.clone
  158.2 0.0 copy-done.1
  158.2 0.6 while.14
  158.8 0.1 reshape.91
  158.9 0.7 copy.38
  159.6 34.3 %all-to-all-start.1 = ((f32[64,16,4]{1,2,0:T(4,128)}), f32[64,16,4]{1,2,0:T(4,128)S(1)}, u32[]{:S(2)}, u32[]{:S(2)}) async-start(f32[64,16,4]{1,2,0:T(4,128)} %copy.38), calls=%async_computation.1 | async-start | bytes 262144 | tf_op jit(solution)/shard_map/all_to_all | solution.py:108
  194.0 0.1 reshape.92
  194.1 0.1 copy.41
  194.2 9.8 %all-to-all-done.1 = f32[64,16,4]{1,2,0:T(4,128)S(1)} async-done(((f32[64,16,4]{1,2,0:T(4,128)}), f32[64,16,4]{1,2,0:T(4,128)S(1)}, u32[]{:S(2)}, u32[]{:S(2)}) %all-to-all-start.1) | async-done | bytes 16416 | tf_op jit(solution)/shard_map/all_to_all | solution.py:108
  204.0 14.3 %all_to_all.15 = f32[64,16,4]{1,2,0:T(4,128)S(1)} all-to-all(f32[64,16,4]{1,2,0:T(4,128)S(1)} %copy.41), channel_id=1, replica_groups=mesh['tensor'=8,'ctx'=64] {'ctx'}, dimensions={0} | all-to-all | bytes 32768 | tf_op jit(solution)/shard_map/all_to_all | solution.py:111
  218.3 5.5 %all-to-all-start = ((f32[64,16,384]{2,1,0:T(8,128)}), f32[64,16,384]{2,1,0:T(8,128)}, u32[]{:S(2)}, u32[]{:S(2)}) async-start(f32[64,16,384]{2,1,0:T(8,128)} %bitcast.73), calls=%async_computation | async-start | bytes 3145728 | tf_op jit(solution)/shard_map/all_to_all | solution.py:105
  223.8 0.0 all-reduce.2.cloned.1.call-start
  223.8 0.1 copy.39
  223.9 0.1 reduce_max.18
  224.0 0.1 copy.42
  224.1 0.2 multiply_reduce_fusion.2
  224.3 0.3 copy.40
  224.6 1.2 mul.75
  225.9 2.2 mul.76
  228.0 0.1 copy.44
  228.1 0.1 div.14
  228.2 0.1 div.15
  228.3 23.0 %all-to-all-done = f32[64,16,384]{2,1,0:T(8,128)} async-done(((f32[64,16,384]{2,1,0:T(8,128)}), f32[64,16,384]{2,1,0:T(8,128)}, u32[]{:S(2)}, u32[]{:S(2)}) %all-to-all-start) | async-done | bytes 1572896 | tf_op jit(solution)/shard_map/all_to_all | solution.py:105
  251.3 2.1 multiply_reduce_fusion
  253.4 0.0 copy-start
  253.4 22.1 %all-gather.2.cloned.1.call-done = bf16[384,3072]{0,1:T(8,128)(2,1)} async-done(((bf16[384,48]{0,1:T(8,128)(2,1)}), bf16[384,3072]{0,1:T(8,128)(2,1)}) %all-gather.2.cloned.1.call-update) | async-done | bytes 2359312 | tf_op jit(solution)/shard_map/all_gather | solution.py:124
  275.5 3.0 convolution_convert_fusion
  278.5 0.0 all-reduce.2.cloned.1.call-update
  278.6 118.6 %all-reduce.2.cloned.1.call-done = bf16[16,3072]{1,0:T(8,128)(2,1)} async-done(((bf16[16,3072]{1,0:T(8,128)(2,1)}), bf16[16,3072]{1,0:T(8,128)(2,1)}) %all-reduce.2.cloned.1.call-update) | async-done | bytes 98320 | tf_op jit(solution)/shard_map/psum | solution.py:128
  397.2 1.0 multiply_reduce_fusion.1
  398.2 0.9 convert_element_type.21
  399.1 0.0 copy-done
  399.2 0.7 multiply_convert_fusion
  (5 shorter events, 0.0 us)
Async XLA Ops:
  6.5 151.6 %copy-start.1 = (s32[4]{0:T(128)S(1)}, s32[4]{0:T(128)}, u32[]{:S(2)}) copy-start(s32[4]{0:T(128)} %param.12) | copy-start | bytes 52
  6.5 269.0 %all-gather.2.cloned.1.call-start = ((), (), s32[]{:S(2)}) async-start(), calls=%async_computation.3 | async-start | bytes 2396160 | tf_op jit(solution)/shard_map/all_gather | solution.py:124
  159.6 44.4 %all-to-all-start.1 = ((f32[64,16,4]{1,2,0:T(4,128)}), f32[64,16,4]{1,2,0:T(4,128)S(1)}, u32[]{:S(2)}, u32[]{:S(2)}) async-start(f32[64,16,4]{1,2,0:T(4,128)} %copy.38), calls=%async_computation.1 | async-start | bytes 262144 | tf_op jit(solution)/shard_map/all_to_all | solution.py:108
  218.3 33.0 %all-to-all-start = ((f32[64,16,384]{2,1,0:T(8,128)}), f32[64,16,384]{2,1,0:T(8,128)}, u32[]{:S(2)}, u32[]{:S(2)}) async-start(f32[64,16,384]{2,1,0:T(8,128)} %bitcast.73), calls=%async_computation | async-start | bytes 3145728 | tf_op jit(solution)/shard_map/all_to_all | solution.py:105
  223.8 173.4 %all-reduce.2.cloned.1.call-start = ((), (), s32[]{:S(2)}) async-start(), calls=%async_computation.4 | async-start | bytes 196608 | tf_op jit(solution)/shard_map/psum | solution.py:128
  253.4 145.8 %copy-start = (f32[384]{0:T(512)S(1)}, f32[384]{0:T(512)}, u32[]{:S(2)}) copy-start(f32[384]{0:T(512)} %param.15) | copy-start | bytes 4612
Sparse Core Ops, SparseCore 0:
  9.4 266.0 all-gather.1
  278.7 118.4 all-reduce.1
where the time goes:
time: 408 us; the launch traced here: 407 us
  waiting for transfers between devices  174 us (43%)
  blocking collectives  161 us (39%)
  starting transfers between devices  39.9 us (10%)
  between operations  13.5 us (3%)
  other arithmetic  7.99 us (2%)
  local copies, waits for them, and re-layouts  6.47 us (2%)
    all_gather x1, blocking collectives, body(): gathered = lax.all_gather(queries, 'ctx', axis=0, tiled=True)  147 us
    psum x1, waiting for transfers between devices, body(): lax.psum(proj.astype(jnp.bfloat16), 'tensor').astype(jnp.float32)  119 us
    all_to_all x1, starting transfers between devices, body(): lax.all_to_all(top_acc.reshape(n_ctx, own_rows, heads_dev), 'ctx', split_...  34.3 us
    all_to_all x1, waiting for transfers between devices, body(): lax.all_to_all(out_sum.reshape(n_ctx, own_rows, features), 'ctx', split_a...  23 us
    all_gather x1, waiting for transfers between devices, body(): lax.all_gather(out_weight, 'ctx', axis=1, tiled=True)  22.1 us
    all_to_all x1, blocking collectives, body(): lax.all_to_all(mass_acc.reshape(n_ctx, own_rows, heads_dev), 'ctx', split...  14.3 us
    all_to_all x1, waiting for transfers between devices, body(): lax.all_to_all(top_acc.reshape(n_ctx, own_rows, heads_dev), 'ctx', split_...  9.84 us
  transfers between devices with their start and end apart: 4, of which 4 were waited for; matrix products, arithmetic and copies ran while one was open for 3% of the time, Pallas kernels for 0%

commit v1 on v0

v1 whole, which is shorter than its diff:
```python
import functools
import math

import jax
import jax.numpy as jnp
from jax import lax
from jax.experimental import pallas as pl
from jax.experimental.pallas import tpu as pltpu
from jax.sharding import PartitionSpec as P

HD = 96
REQS = 4
HEADS_DEV = 4
FEATS = 384
SPAN = 256
PLANE = 16
ROWS = 16
YS = 8
GROUPS = 8
D = 3072
NEG = -1e30
WIDE = FEATS + 128


def remote(src, dst, send, recv, device):
    return pltpu.make_async_remote_copy(
        src_ref=src,
        dst_ref=dst,
        send_sem=send,
        recv_sem=recv,
        device_id=device,
        device_id_type=pl.DeviceIdType.MESH,
    )


def signal(sem, device):
    pl.semaphore_signal(sem, inc=1, device_id=device, device_id_type=pl.DeviceIdType.MESH)


def gather_kernel(q_ref, out_ref, own_sem, send_plane, send_x, recv):
    me = lax.axis_index("ctx")
    x, j = me // PLANE, me % PLANE
    barrier = pltpu.get_barrier_semaphore()

    def greet(k, c):
        signal(barrier, {"ctx": x * PLANE + (j + k) % PLANE})
        return c

    lax.fori_loop(1, PLANE, greet, 0)
    for dx in range(1, REQS):
        signal(barrier, {"ctx": (x + dx) % REQS * PLANE + j})
    own = pltpu.make_async_copy(q_ref, out_ref.at[me], own_sem)
    own.start()
    pl.semaphore_wait(barrier, PLANE - 1 + REQS - 1)

    def to_plane(k):
        there = x * PLANE + (j + k) % PLANE
        return remote(q_ref, out_ref.at[me], send_plane.at[k], recv.at[me], {"ctx": there})

    def to_x(k, dx):
        block = x * PLANE + (j + PLANE - k) % PLANE
        there = (x + dx) % REQS * PLANE + j
        src = q_ref if isinstance(k, int) and k == 0 else out_ref.at[block]
        return remote(
            src, out_ref.at[block], send_x.at[dx - 1, k], recv.at[block], {"ctx": there}
        )

    def start_plane(k, c):
        to_plane(k).start()
        return c

    for dx in range(1, REQS):
        to_x(0, dx).start()
    lax.fori_loop(1, PLANE, start_plane, 0)

    def forward(k, c):
        block = x * PLANE + (j + PLANE - k) % PLANE
        pltpu.make_async_copy(out_ref.at[block], out_ref.at[block], recv.at[block]).wait()
        for dx in range(1, REQS):
            to_x(k, dx).start()
        return c

    lax.fori_loop(1, PLANE, forward, 0)

    def arrive(k, c):
        for dx in range(1, REQS):
            block = (x + dx) % REQS * PLANE + (j + PLANE - k) % PLANE
            pltpu.make_async_copy(out_ref.at[block], out_ref.at[block], recv.at[block]).wait()
        return c

    lax.fori_loop(0, PLANE, arrive, 0)

    def sent(k, c):
        to_plane(k).wait_send()
        for dx in range(1, REQS):
            to_x(k, dx).wait_send()
        return c

    lax.fori_loop(1, PLANE, sent, 0)
    for dx in range(1, REQS):
        to_x(0, dx).wait_send()
    own.wait()


def split_parts(lse):
    lane = lax.broadcasted_iota(jnp.int32, lse.shape, 1)
    high = lse.astype(jnp.bfloat16).astype(jnp.float32)
    rest = lse - high
    mid = rest.astype(jnp.bfloat16).astype(jnp.float32)
    low = rest - mid
    part = lane % 4
    picked = jnp.where(part == 0, high, jnp.where(part == 1, mid, jnp.where(part == 2, low, 0.0)))
    return jnp.where(lane < 4 * HEADS_DEV, picked, 0.0).astype(jnp.bfloat16)


def attention_kernel(table_ref, len_ref, q_ref, k_ref, v_ref, out_ref):
    slots = k_ref.shape[0]
    block_rows = k_ref.shape[1]
    me = lax.axis_index("ctx")
    scale = 1.0 / math.sqrt(HD)
    empty_parts = split_parts(jnp.full((SPAN, 128), NEG, jnp.float32))
    for r in range(REQS):
        out_ref[r, :, :FEATS] = jnp.zeros((SPAN, FEATS), jnp.bfloat16)
        out_ref[r, :, FEATS:] = empty_parts
    before = None
    for s in range(slots):
        slot_id = me * slots + s
        found = jnp.int32(-1)
        for r in range(REQS):
            for b in range(table_ref.shape[1]):
                found = jnp.where(table_ref[r, b] == slot_id, r * 16 + b, found)
        used = found >= 0
        request = jnp.where(used, found // 16, 0)
        first_key = jnp.where(used, found % 16 * block_rows, 1 << 28)
        diff = (
            lax.broadcasted_iota(jnp.int32, (SPAN, block_rows), 1)
            - lax.broadcasted_iota(jnp.int32, (SPAN, block_rows), 0)
        )
        visible = diff <= len_ref[request] - first_key
        query = q_ref[pl.ds(pl.multiple_of(request * SPAN, SPAN), SPAN), :]
        tiles = [jnp.zeros((SPAN, 128), jnp.float32) for _ in range(FEATS // 128)]
        lane = lax.broadcasted_iota(jnp.int32, (SPAN, 128), 1)
        lse = jnp.full((SPAN, 128), NEG, jnp.float32)
        for h in range(HEADS_DEV):
            first, last = h * HD // 128, (h * HD + HD + 127) // 128
            lo, hi = first * 128, last * 128
            col = lo + lax.broadcasted_iota(jnp.int32, (SPAN, hi - lo), 1)
            mine = (col >= h * HD) & (col < h * HD + HD)
            part = query[:, lo:hi]
            part = jnp.where(mine, part, jnp.zeros_like(part))
            scores = lax.dot_general(
                part, k_ref[s, :, lo:hi], (((1,), (1,)), ((), ())),
                preferred_element_type=jnp.float32,
            ) * scale
            scores = jnp.where(visible, scores, NEG)
            top = jnp.max(scores, axis=1, keepdims=True)
            weights = jnp.where(visible, jnp.exp(scores - top), 0.0)
            total = jnp.sum(weights, axis=1, keepdims=True)
            mixed = jnp.dot(
                weights.astype(jnp.bfloat16), v_ref[s, :, lo:hi],
                preferred_element_type=jnp.float32,
            )
            some = total > 0.0
            safe = jnp.where(some, total, 1.0)
            mixed = jnp.where(mine, mixed * (1.0 / safe), 0.0)
            for t in range(first, last):
                tiles[t] = tiles[t] + mixed[:, t * 128 - lo : t * 128 - lo + 128]
            level = jnp.where(some, top + jnp.log(safe), NEG)
            lse = jnp.where(lane // 4 == h, level, lse)
        if before is None:
            before = (used, request)

            @pl.when(used)
            def _():
                for t in range(FEATS // 128):
                    out_ref[request, :, t * 128 : t * 128 + 128] = tiles[t].astype(jnp.bfloat16)
                out_ref[request, :, FEATS:] = split_parts(lse)

            first_tiles, first_lse = tiles, lse
        else:
            same = before[0] & used & (before[1] == request)
            held = jnp.where(same, first_lse, NEG)
            best = jnp.maximum(held, lse)
            keep, take = jnp.exp(held - best), jnp.exp(lse - best)
            mass = keep + take
            keep, take = keep / mass, take / mass
            level = best + jnp.log(mass)

            @pl.when(used)
            def _():
                for t in range(FEATS // 128):
                    col = t * 128 + lane
                    k_b = jnp.zeros((SPAN, 128), jnp.float32)
                    t_b = jnp.zeros((SPAN, 128), jnp.float32)
                    for h in range(HEADS_DEV):
                        if h * HD < t * 128 + 128 and h * HD + HD > t * 128:
                            mine = (col >= h * HD) & (col < h * HD + HD)
                            k_b = jnp.where(mine, keep[:, 4 * h : 4 * h + 1], k_b)
                            t_b = jnp.where(mine, take[:, 4 * h : 4 * h + 1], t_b)
                    merged = first_tiles[t] * k_b + tiles[t] * t_b
                    out_ref[request, :, t * 128 : t * 128 + 128] = merged.astype(jnp.bfloat16)
                out_ref[request, :, FEATS:] = split_parts(level)


def spread(columns, width):
    row = lax.broadcasted_iota(jnp.int32, (128, columns), 0)
    col = lax.broadcasted_iota(jnp.int32, (128, columns), 1)
    hit = (row // 4 == col // width) & (row < 4 * HEADS_DEV)
    return jnp.where(hit, 1.0, 0.0).astype(jnp.bfloat16)


def finish_kernel(
    part_ref, w_ref, gain_ref, out_ref,
    recv_a, comb, recv_b, w_all, attn_own, attn_all, proj, recv_p, ssq_own, recv_s,
    sa_send, sa_recv, sb_send, sb_recv, sw_send, sw_recv, sg_send, sg_recv,
    sp_send, sp_recv, ss_send, ss_recv, diag_sem,
):
    me = lax.axis_index("ctx")
    tensor = lax.axis_index("tensor")
    x, j = me // PLANE, me % PLANE
    group, y = me // YS, me % YS
    barrier = pltpu.get_barrier_semaphore()
    off_diag = group != tensor

    def greet_plane(k, c):
        signal(barrier, {"ctx": x * PLANE + (j + k) % PLANE})
        return c

    def greet_eight(k, c):
        signal(barrier, {"ctx": (group + k) % GROUPS * YS + y})
        signal(barrier, {"tensor": (tensor + k) % GROUPS})
        signal(barrier, {"tensor": (group + GROUPS - k) % GROUPS, "ctx": tensor * YS + y})
        return c

    lax.fori_loop(1, PLANE, greet_plane, 0)
    lax.fori_loop(1, GROUPS, greet_eight, 0)

    @pl.when(off_diag)
    def _():
        signal(barrier, {"tensor": group, "ctx": tensor * YS + y})

    pl.semaphore_wait(barrier, PLANE - 1 + 3 * (GROUPS - 1) + off_diag.astype(jnp.int32))

    def to_x(dx):
        there = (x + dx) % REQS
        return remote(
            part_ref.at[there], recv_a.at[dx - 1], sa_send.at[dx - 1], sa_recv.at[dx - 1],
            {"ctx": there * PLANE + j},
        )

    for dx in range(1, REQS):
        to_x(dx).start()

    def to_y(k):
        return remote(
            w_ref, w_all.at[y], sw_send.at[k], sw_recv.at[k], {"ctx": group * YS + (y + k) % YS}
        )

    def start_y(k, c):
        to_y(k).start()
        return c

    lax.fori_loop(1, YS, start_y, 0)
    own_w = pltpu.make_async_copy(w_ref, w_all.at[y], diag_sem)
    own_w.start()

    to_heads = spread(FEATS, HD)
    to_lanes = spread(128, 4)

    def level_of(parts, pick):
        return jnp.dot(parts, pick, preferred_element_type=jnp.float32)

    for dx in range(1, REQS):
        to_x(dx).wait_recv()

    def to_plane(k):
        there = x * PLANE + (j + k) % PLANE
        return remote(comb.at[k], recv_b.at[k], sb_send.at[k], sb_recv.at[k], {"ctx": there})

    def combine(k):
        rows = pl.ds(pl.multiple_of((j + k) % PLANE * ROWS, ROWS), ROWS)
        blocks = [part_ref[x, rows, :]] + [recv_a[i, rows, :] for i in range(REQS - 1)]
        parts = [b[:, FEATS:] for b in blocks]
        wide = [level_of(p, to_heads) for p in parts]
        best = functools.reduce(jnp.maximum, wide)
        factors = [jnp.exp(w - best) for w in wide]
        mass = sum(factors)
        mixed = sum(b[:, :FEATS].astype(jnp.float32) * f for b, f in zip(blocks, factors))
        narrow = [level_of(p, to_lanes) for p in parts]
        top = functools.reduce(jnp.maximum, narrow)
        level = top + jnp.log(sum(jnp.exp(n - top) for n in narrow))
        return (mixed / mass).astype(jnp.bfloat16), split_parts(level)

    def reduce_x(k, c):
        mixed, parts = combine(k)
        comb[k, :, :FEATS] = mixed
        comb[k, :, FEATS:] = parts
        to_plane(k).start()
        return c

    lax.fori_loop(1, PLANE, reduce_x, 0)
    own_mixed, own_parts = combine(0)
    recv_b[0, :, :FEATS] = own_mixed
    recv_b[0, :, FEATS:] = own_parts

    def arrive_b(k, c):
        to_plane(k).wait_recv()
        return c

    lax.fori_loop(1, PLANE, arrive_b, 0)
    levels = level_of(recv_b[:, :, FEATS:].reshape(PLANE * ROWS, 128), to_heads)
    levels = levels.reshape(PLANE, ROWS, FEATS)
    best = jnp.max(levels, axis=0)
    factors = jnp.exp(levels - best[None])
    mass = jnp.sum(factors, axis=0)
    mixed = jnp.sum(recv_b[:, :, :FEATS].astype(jnp.float32) * factors, axis=0)
    attn = (mixed / mass).astype(jnp.bfloat16)
    attn_own[...] = attn

    def to_group(k):
        return remote(
            attn_own, attn_all.at[group], sg_send.at[k], sg_recv.at[k],
            {"ctx": (group + k) % GROUPS * YS + y},
        )

    def start_group(k, c):
        to_group(k).start()
        return c

    lax.fori_loop(1, GROUPS, start_group, 0)
    attn_all[group] = attn
    own_w.wait()

    def arrive_g(k, c):
        to_y(k).wait_recv()
        to_group(k).wait_recv()
        return c

    lax.fori_loop(1, GROUPS, arrive_g, 0)
    partial = lax.dot_general(
        attn_all[...].reshape(GROUPS * ROWS, FEATS), w_all[...].reshape(FEATS, FEATS),
        (((1,), (1,)), ((), ())), preferred_element_type=jnp.float32,
    )
    proj[...] = partial.astype(jnp.bfloat16).reshape(GROUPS, ROWS, FEATS)

    def to_owner(k):
        there = (tensor + k) % GROUPS
        return remote(
            proj.at[there], recv_p.at[k], sp_send.at[k], sp_recv.at[k],
            {"tensor": group, "ctx": there * YS + y},
        )

    def start_owner(k, c):
        to_owner(k).start()
        return c

    lax.fori_loop(1, GROUPS, start_owner, 0)

    @pl.when(off_diag)
    def _():
        to_owner(0).start()
        to_owner(0).wait_recv()

    @pl.when(jnp.logical_not(off_diag))
    def _():
        recv_p[0] = proj[tensor]

    def arrive_p(k, c):
        to_owner(k).wait_recv()
        return c

    lax.fori_loop(1, GROUPS, arrive_p, 0)
    summed = jnp.sum(recv_p[...].astype(jnp.float32), axis=0)
    squares = jnp.broadcast_to(jnp.sum(summed * summed, axis=1, keepdims=True), (ROWS, 128))
    ssq_own[...] = squares

    def to_tensor(k):
        return remote(
            ssq_own, recv_s.at[k], ss_send.at[k], ss_recv.at[k],
            {"tensor": (tensor + k) % GROUPS},
        )

    def start_tensor(k, c):
        to_tensor(k).start()
        return c

    lax.fori_loop(1, GROUPS, start_tensor, 0)
    recv_s[0] = squares

    def arrive_s(k, c):
        to_tensor(k).wait_recv()
        return c

    lax.fori_loop(1, GROUPS, arrive_s, 0)
    total = jnp.sum(recv_s[...], axis=0)[:, :1]
    inverse = lax.rsqrt(total * (1.0 / D) + 1e-05)
    out_ref[...] = (summed * inverse * gain_ref[...]).astype(jnp.bfloat16)

    for dx in range(1, REQS):
        to_x(dx).wait_send()

    def sent_plane(k, c):
        to_plane(k).wait_send()
        return c

    def sent_eight(k, c):
        to_y(k).wait_send()
        to_group(k).wait_send()
        to_owner(k).wait_send()
        to_tensor(k).wait_send()
        return c

    lax.fori_loop(1, PLANE, sent_plane, 0)
    lax.fori_loop(1, GROUPS, sent_eight, 0)

    @pl.when(off_diag)
    def _():
        to_owner(0).wait_send()


def body(queries, key_cache, value_cache, cached_len, block_slot, out_weight, norm_gain):
    vmem = pl.BlockSpec(memory_space=pltpu.VMEM)
    smem = pl.BlockSpec(memory_space=pltpu.SMEM)
    dma = pltpu.SemaphoreType.DMA
    bf16, f32 = jnp.bfloat16, jnp.float32
    n_ctx = REQS * PLANE
    weight_rows = out_weight.T
    gathered = pl.pallas_call(
        gather_kernel,
        out_shape=jax.ShapeDtypeStruct((n_ctx, ROWS, FEATS), bf16),
        in_specs=[vmem],
        out_specs=vmem,
        scratch_shapes=[dma, dma((PLANE,)), dma((REQS - 1, PLANE)), dma((n_ctx,))],
        compiler_params=pltpu.CompilerParams(collective_id=0, has_side_effects=True),
        name="gather_queries",
    )(queries)
    parts = pl.pallas_call(
        attention_kernel,
        out_shape=jax.ShapeDtypeStruct((REQS, SPAN, WIDE), bf16),
        in_specs=[smem, smem, vmem, vmem, vmem],
        out_specs=vmem,
        name="attention",
    )(block_slot, cached_len, gathered.reshape(n_ctx * ROWS, FEATS), key_cache, value_cache)
    return pl.pallas_call(
        finish_kernel,
        out_shape=jax.ShapeDtypeStruct((ROWS, FEATS), bf16),
        in_specs=[vmem] * 3,
        out_specs=vmem,
        scratch_shapes=[
            pltpu.VMEM((REQS - 1, SPAN, WIDE), bf16),
            pltpu.VMEM((PLANE, ROWS, WIDE), bf16),
            pltpu.VMEM((PLANE, ROWS, WIDE), bf16),
            pltpu.VMEM((YS, FEATS // YS, FEATS), bf16),
            pltpu.VMEM((ROWS, FEATS), bf16),
            pltpu.VMEM((GROUPS, ROWS, FEATS), bf16),
            pltpu.VMEM((GROUPS, ROWS, FEATS), bf16),
            pltpu.VMEM((GROUPS, ROWS, FEATS), bf16),
            pltpu.VMEM((ROWS, 128), f32),
            pltpu.VMEM((GROUPS, ROWS, 128), f32),
            dma((REQS - 1,)), dma((REQS - 1,)),
            dma((PLANE,)), dma((PLANE,)),
            dma((YS,)), dma((YS,)),
            dma((GROUPS,)), dma((GROUPS,)),
            dma((GROUPS,)), dma((GROUPS,)),
            dma((GROUPS,)), dma((GROUPS,)),
            dma,
        ],
        compiler_params=pltpu.CompilerParams(collective_id=1, has_side_effects=True),
        name="merge_project_norm",
    )(parts, weight_rows, norm_gain.reshape(1, FEATS))


def solution(mesh):
    in_specs = (
        P("ctx", "tensor"),
        P("ctx", None, "tensor"),
        P("ctx", None, "tensor"),
        P(),
        P(),
        P("tensor", "ctx"),
        P("tensor"),
    )
    out_specs = P("ctx", "tensor")
    return jax.shard_map(body, mesh=mesh, in_specs=in_specs, out_specs=out_specs, check_vma=False)
```

time: 408 us -> 88.4 us (0.22)
  waiting for transfers between devices: 174 us -> 0 us
  blocking collectives: 161 us -> 0 us
  Pallas kernels: 0 us -> 86.2 us
  starting transfers between devices: 39.9 us -> 0 us
  between operations: 13.5 us -> 0.03 us
  other arithmetic: 7.99 us -> 0 us
  local copies, waits for them, and re-layouts: 6.47 us -> 1.88 us
    all_gather x1 -> x0, blocking collectives: 147 us -> none  [body(): gathered = lax.all_gather(queries, 'ctx', axis=0, tiled=True)]
    psum x1 -> x0, waiting for transfers between devices: 119 us -> none  [body(): lax.psum(proj.astype(jnp.bfloat16), 'tensor').astype(jnp.float32)]
    pallas_call x0 -> x3, Pallas kernels: none -> 86.2 us  [the longest x1 57.2 us: body(): pl.pallas_call(finish_kernel, out_shape=jax.ShapeDtypeStruct((ROWS, FEATS...]
    all_to_all x2 -> x0, starting transfers between devices: 39.8 us -> none  [the longest x1 34.3 us: body(): lax.all_to_all(top_acc.reshape(n_ctx, own_rows, heads_dev), 'ctx', split_...]
    all_to_all x2 -> x0, waiting for transfers between devices: 32.9 us -> none  [the longest x1 23 us: body(): lax.all_to_all(out_sum.reshape(n_ctx, own_rows, features), 'ctx', split_a...]
    all_gather x1 -> x0, waiting for transfers between devices: 22.1 us -> none  [body(): lax.all_gather(out_weight, 'ctx', axis=1, tiled=True)]
    all_to_all x1 -> x0, blocking collectives: 14.3 us -> none  [body(): lax.all_to_all(mass_acc.reshape(n_ctx, own_rows, heads_dev), 'ctx', split...]
    reduce_sum x4 -> x0, other arithmetic: 4.18 us -> none  [the longest x1 2.05 us: body(): jnp.sum(outs.reshape(sources, items, heads_dev, HD) * factor[:, :, :, Non...]
  transfers between devices with their start and end apart: 4 -> 0, of which waited for: 4 -> 0; matrix products, arithmetic and copies ran while one was open for 3% -> 0% of each run, Pallas kernels for 0% -> 0%
where the time goes in v1:
time: 88.4 us; the launch traced here: 88.1 us
  Pallas kernels  86.2 us (98%)
  local copies, waits for them, and re-layouts  1.88 us (2%)
    pallas_call x1, Pallas kernels, body(): pl.pallas_call(finish_kernel, out_shape=jax.ShapeDtypeStruct((ROWS, FEATS...  57.2 us
    pallas_call x1, Pallas kernels, body(): pl.pallas_call(gather_kernel, out_shape=jax.ShapeDtypeStruct((n_ctx, ROWS...  23 us
    pallas_call x1, Pallas kernels, body(): pl.pallas_call(attention_kernel, out_shape=jax.ShapeDtypeStruct((REQS, SP...  5.99 us

profile of v1, /device:TPU:1, one launch (start us, length us, event | category | flops | bytes accessed | tf_op | source)
XLA Modules:
  0.0 88.1 jit_solution(4307556853857615470)
XLA Ops:
  0.0 23.0 %gather_queries.1 = bf16[64,16,384]{2,1,0:T(8,128)(2,1)} custom-call(bf16[16,384]{1,0:T(8,128)(2,1)} %q_ref.1), custom_call_target="tpu_custom_call" | custom-call | tf_op jit(solution)/shard_map/gather_queries/pallas_call | solution.py:428
  23.0 0.0 copy-start
  23.0 6.0 %attention.1.part_ref = bf16[4,256,512]{2,1,0:T(8,128)(2,1)} custom-call(s32[4,16]{1,0:T(4,128)} %table_ref.1, s32[4]{0:T(128)} %len_ref.1, bf16[1024,384]{1,0:T(8,128)(2,1)} %bitcast.2, bf16[2,512,384]{2,1,0:T(8,128)(2,1)} %k_ref.1, bf16[2,512,384]{2,1,0:T(8,128)(2,1)} %v_ref.1), custom_call_target="tpu_custom_call" | custom-call | tf_op jit(solution)/shard_map/attention/pallas_call | solution.py:437
  29.0 0.0 copy-done
  29.0 0.6 reshape.7.gain_ref
  29.6 57.2 %merge_project_norm.1 = bf16[16,384]{1,0:T(8,128)(2,1)} custom-call(bf16[4,256,512]{2,1,0:T(8,128)(2,1)} %attention.1.part_ref, bf16[48,384]{1,0:T(8,128)(2,1)} %bitcast.3, f32[1,384]{1,0:T(1,128)} %reshape.7.gain_ref), custom_call_target="tpu_custom_call" | custom-call | tf_op jit(solution)/shard_map/merge_project_norm/pallas_call | solution.py:444
  86.8 1.3 %copy.9 = bf16[16,384]{1,0:T(8,128)(2,1)} copy(bf16[16,384]{1,0:T(8,128)(2,1)} %merge_project_norm.1) | data formatting | bytes 24576
Async XLA Ops:
  23.0 6.0 %copy-start = (f32[384]{0:T(512)S(1)}, f32[384]{0:T(512)}, u32[]{:S(2)}) copy-start(f32[384]{0:T(512)} %param.13) | copy-start | bytes 4612

commit v2 on v1

--- a/solution.py
+++ b/solution.py
@@ -37,9 +37,10 @@
     pl.semaphore_signal(sem, inc=1, device_id=device, device_id_type=pl.DeviceIdType.MESH)
 
 
-def gather_kernel(q_ref, out_ref, own_sem, send_plane, send_x, recv):
+def gather_kernel(q_ref, out_ref, own_sem, send_plane, send_near, send_far, recv):
     me = lax.axis_index("ctx")
     x, j = me // PLANE, me % PLANE
+    up, down = (x + 1) % REQS, (x + REQS - 1) % REQS
     barrier = pltpu.get_barrier_semaphore()
 
     def greet(k, c):
@@ -47,58 +48,87 @@
         return c
 
     lax.fori_loop(1, PLANE, greet, 0)
-    for dx in range(1, REQS):
-        signal(barrier, {"ctx": (x + dx) % REQS * PLANE + j})
+    for there in (up, down):
+        signal(barrier, {"ctx": there * PLANE + j})
     own = pltpu.make_async_copy(q_ref, out_ref.at[me], own_sem)
     own.start()
-    pl.semaphore_wait(barrier, PLANE - 1 + REQS - 1)
+    pl.semaphore_wait(barrier, PLANE - 1 + 2)
+
+    def block_of(plane, k):
+        return plane * PLANE + (j + PLANE - k) % PLANE
 
     def to_plane(k):
         there = x * PLANE + (j + k) % PLANE
         return remote(q_ref, out_ref.at[me], send_plane.at[k], recv.at[me], {"ctx": there})
 
-    def to_x(k, dx):
-        block = x * PLANE + (j + PLANE - k) % PLANE
-        there = (x + dx) % REQS * PLANE + j
-        src = q_ref if isinstance(k, int) and k == 0 else out_ref.at[block]
-        return remote(
-            src, out_ref.at[block], send_x.at[dx - 1, k], recv.at[block], {"ctx": there}
-        )
+    def pass_on(plane, there, k, sem):
+        block = block_of(plane, k)
+        src = q_ref if isinstance(k, int) and k == 0 and plane is x else out_ref.at[block]
+        return remote(src, out_ref.at[block], sem, recv.at[block], {"ctx": there * PLANE + j})
+
+    def near(k):
+        return [pass_on(x, up, k, send_near.at[0, k]), pass_on(x, down, k, send_near.at[1, k])]
+
+    def far(i):
+        return [
+            pass_on(down, up, 2 * i, send_far.at[2 * i]),
+            pass_on(up, down, 2 * i + 1, send_far.at[2 * i + 1]),
+        ]
+
+    def arrived(plane, k):
+        block = block_of(plane, k)
+        pltpu.make_async_copy(out_ref.at[block], out_ref.at[block], recv.at[block]).wait()
 
     def start_plane(k, c):
         to_plane(k).start()
         return c
 
-    for dx in range(1, REQS):
-        to_x(0, dx).start()
+    for copy in near(0):
+        copy.start()
     lax.fori_loop(1, PLANE, start_plane, 0)
 
-    def forward(k, c):
-        block = x * PLANE + (j + PLANE - k) % PLANE
-        pltpu.make_async_copy(out_ref.at[block], out_ref.at[block], recv.at[block]).wait()
-        for dx in range(1, REQS):
-            to_x(k, dx).start()
-        return c
-
-    lax.fori_loop(1, PLANE, forward, 0)
-
-    def arrive(k, c):
-        for dx in range(1, REQS):
-            block = (x + dx) % REQS * PLANE + (j + PLANE - k) % PLANE
-            pltpu.make_async_copy(out_ref.at[block], out_ref.at[block], recv.at[block]).wait()
-        return c
-
-    lax.fori_loop(0, PLANE, arrive, 0)
+    def forward(k):
+        arrived(x, k)
+        for copy in near(k):
+            copy.start()
+
+    def relay(i):
+        arrived(down, 2 * i)
+        far(i)[0].start()
+        arrived(up, 2 * i + 1)
+        far(i)[1].start()
+
+    forward(1)
+
+    def step(i, c):
+        forward(2 * i)
+        forward(2 * i + 1)
+        relay(i - 1)
+        return c
+
+    lax.fori_loop(1, PLANE // 2, step, 0)
+    relay(PLANE // 2 - 1)
+
+    def rest(i, c):
+        arrived(down, 2 * i + 1)
+        arrived(up, 2 * i)
+        arrived((x + 2) % REQS, 2 * i)
+        arrived((x + 2) % REQS, 2 * i + 1)
+        for copy in far(i):
+            copy.wait_send()
+        return c
+
+    lax.fori_loop(0, PLANE // 2, rest, 0)
 
     def sent(k, c):
         to_plane(k).wait_send()
-        for dx in range(1, REQS):
-            to_x(k, dx).wait_send()
+        for copy in near(k):
+            copy.wait_send()
         return c
 
     lax.fori_loop(1, PLANE, sent, 0)
-    for dx in range(1, REQS):
-        to_x(0, dx).wait_send()
+    for copy in near(0):
+        copy.wait_send()
     own.wait()
 
 
@@ -211,8 +241,8 @@
 
 def finish_kernel(
     part_ref, w_ref, gain_ref, out_ref,
-    recv_a, comb, recv_b, w_all, attn_own, attn_all, proj, recv_p, ssq_own, recv_s,
-    sa_send, sa_recv, sb_send, sb_recv, sw_send, sw_recv, sg_send, sg_recv,
+    relay_in, relay_out, recv_a, comb, recv_b, w_all, attn_own, attn_all, proj, recv_p, ssq_own, recv_s,
+    sr_send, sr_recv, sa_send, sa_recv, sb_send, sb_recv, sw_send, sw_recv, sg_send, sg_recv,
     sp_send, sp_recv, ss_send, ss_recv, diag_sem,
 ):
     me = lax.axis_index("ctx")
@@ -241,15 +271,38 @@
 
     pl.semaphore_wait(barrier, PLANE - 1 + 3 * (GROUPS - 1) + off_diag.astype(jnp.int32))
 
-    def to_x(dx):
-        there = (x + dx) % REQS
+    half = PLANE // 2
+    toward = ((x + 1) % REQS, (x + REQS - 1) % REQS)
+
+    def rows_of(k):
+        return pl.ds(pl.multiple_of((j + k) % PLANE * ROWS, ROWS), ROWS)
+
+    def to_relay(way, i):
         return remote(
-            part_ref.at[there], recv_a.at[dx - 1], sa_send.at[dx - 1], sa_recv.at[dx - 1],
-            {"ctx": there * PLANE + j},
-        )
-
-    for dx in range(1, REQS):
-        to_x(dx).start()
+            part_ref.at[(x + 2) % REQS, rows_of(2 * i + way)], relay_in.at[way, i],
+            sr_send.at[way, i], sr_recv.at[way, i], {"ctx": toward[way] * PLANE + j},
+        )
+
+    def to_near(way, i, relayed):
+        k = 2 * i + (way if relayed else 1 - way)
+        src = relay_out.at[way, i] if relayed else part_ref.at[toward[way], rows_of(k)]
+        return remote(
+            src, recv_a.at[way, k], sa_send.at[way, k], sa_recv.at[way, k],
+            {"ctx": toward[way] * PLANE + j},
+        )
+
+    def start_relays(t, c):
+        for way in range(2):
+            to_relay(way, (t + 1) % half).start()
+        return c
+
+    def start_near(t, c):
+        for way in range(2):
+            to_near(way, (t + 1) % half, False).start()
+        return c
+
+    lax.fori_loop(0, half, start_relays, 0)
+    lax.fori_loop(0, half, start_near, 0)
 
     def to_y(k):
         return remote(
@@ -270,16 +323,11 @@
     def level_of(parts, pick):
         return jnp.dot(parts, pick, preferred_element_type=jnp.float32)
 
-    for dx in range(1, REQS):
-        to_x(dx).wait_recv()
-
     def to_plane(k):
         there = x * PLANE + (j + k) % PLANE
         return remote(comb.at[k], recv_b.at[k], sb_send.at[k], sb_recv.at[k], {"ctx": there})
 
-    def combine(k):
-        rows = pl.ds(pl.multiple_of((j + k) % PLANE * ROWS, ROWS), ROWS)
-        blocks = [part_ref[x, rows, :]] + [recv_a[i, rows, :] for i in range(REQS - 1)]
+    def combine(blocks):
         parts = [b[:, FEATS:] for b in blocks]
         wide = [level_of(p, to_heads) for p in parts]
         best = functools.reduce(jnp.maximum, wide)
@@ -291,17 +339,48 @@
         level = top + jnp.log(sum(jnp.exp(n - top) for n in narrow))
         return (mixed / mass).astype(jnp.bfloat16), split_parts(level)
 
-    def reduce_x(k, c):
-        mixed, parts = combine(k)
-        comb[k, :, :FEATS] = mixed
-        comb[k, :, FEATS:] = parts
-        to_plane(k).start()
-        return c
-
-    lax.fori_loop(1, PLANE, reduce_x, 0)
-    own_mixed, own_parts = combine(0)
-    recv_b[0, :, :FEATS] = own_mixed
-    recv_b[0, :, FEATS:] = own_parts
+    def relay(t, c):
+        i = (t + 1) % half
+        for way in range(2):
+            to_relay(way, i).wait_recv()
+        merged = [
+            combine([relay_in[way, i], part_ref[toward[way], rows_of(2 * i + way), :]])
+            for way in range(2)
+        ]
+        for way in range(2):
+            relay_out[way, i, :, :FEATS] = merged[way][0]
+            relay_out[way, i, :, FEATS:] = merged[way][1]
+        for way in range(2):
+            to_near(way, i, True).start()
+        return c
+
+    lax.fori_loop(0, half, relay, 0)
+
+    def owned(i):
+        for way in range(2):
+            to_near(way, i, False).wait_recv()
+            to_near(way, i, True).wait_recv()
+        return [
+            combine([part_ref[x, rows_of(k), :], recv_a[0, k], recv_a[1, k]])
+            for k in (2 * i, 2 * i + 1)
+        ]
+
+    def reduce_x(i, c):
+        merged = owned(i)
+        for at in range(2):
+            comb[2 * i + at, :, :FEATS] = merged[at][0]
+            comb[2 * i + at, :, FEATS:] = merged[at][1]
+        for at in range(2):
+            to_plane(2 * i + at).start()
+        return c
+
+    lax.fori_loop(1, half, reduce_x, 0)
+    merged = owned(0)
+    comb[1, :, :FEATS] = merged[1][0]
+    comb[1, :, FEATS:] = merged[1][1]
+    to_plane(1).start()
+    recv_b[0, :, :FEATS] = merged[0][0]
+    recv_b[0, :, FEATS:] = merged[0][1]
 
     def arrive_b(k, c):
         to_plane(k).wait_recv()
@@ -396,8 +475,14 @@
     inverse = lax.rsqrt(total * (1.0 / D) + 1e-05)
     out_ref[...] = (summed * inverse * gain_ref[...]).astype(jnp.bfloat16)
 
-    for dx in range(1, REQS):
-        to_x(dx).wait_send()
+    def sent_a(i, c):
+        for way in range(2):
+            to_relay(way, i).wait_send()
+            to_near(way, i, False).wait_send()
+            to_near(way, i, True).wait_send()
+        return c
+
+    lax.fori_loop(0, half, sent_a, 0)
 
     def sent_plane(k, c):
         to_plane(k).wait_send()
@@ -430,7 +515,7 @@
         out_shape=jax.ShapeDtypeStruct((n_ctx, ROWS, FEATS), bf16),
         in_specs=[vmem],
         out_specs=vmem,
-        scratch_shapes=[dma, dma((PLANE,)), dma((REQS - 1, PLANE)), dma((n_ctx,))],
+        scratch_shapes=[dma, dma((PLANE,)), dma((2, PLANE)), dma((PLANE,)), dma((n_ctx,))],
         compiler_params=pltpu.CompilerParams(collective_id=0, has_side_effects=True),
         name="gather_queries",
     )(queries)
@@ -447,7 +532,9 @@
         in_specs=[vmem] * 3,
         out_specs=vmem,
         scratch_shapes=[
-            pltpu.VMEM((REQS - 1, SPAN, WIDE), bf16),
+            pltpu.VMEM((2, PLANE // 2, ROWS, WIDE), bf16),
+            pltpu.VMEM((2, PLANE // 2, ROWS, WIDE), bf16),
+            pltpu.VMEM((2, PLANE, ROWS, WIDE), bf16),
             pltpu.VMEM((PLANE, ROWS, WIDE), bf16),
             pltpu.VMEM((PLANE, ROWS, WIDE), bf16),
             pltpu.VMEM((YS, FEATS // YS, FEATS), bf16),
@@ -457,7 +544,8 @@
             pltpu.VMEM((GROUPS, ROWS, FEATS), bf16),
             pltpu.VMEM((ROWS, 128), f32),
             pltpu.VMEM((GROUPS, ROWS, 128), f32),
-            dma((REQS - 1,)), dma((REQS - 1,)),
+            dma((2, PLANE // 2)), dma((2, PLANE // 2)),
+            dma((2, PLANE)), dma((2, PLANE)),
             dma((PLANE,)), dma((PLANE,)),
             dma((YS,)), dma((YS,)),
             dma((GROUPS,)), dma((GROUPS,)),

time: 88.4 us -> 89.5 us (1.012)
  Pallas kernels: 86.2 us -> 87.3 us
    pallas_call x1, Pallas kernels: 23 us -> 27.6 us  [body(): pl.pallas_call(gather_kernel, out_shape=jax.ShapeDtypeStruct((n_ctx, ROWS...]
    pallas_call x1, Pallas kernels: 57.2 us -> 53.7 us  [body(): pl.pallas_call(finish_kernel, out_shape=jax.ShapeDtypeStruct((ROWS, FEATS...]
where the time goes in v2:
time: 89.5 us; the launch traced here: 89.2 us
  Pallas kernels  87.3 us (98%)
  local copies, waits for them, and re-layouts  1.88 us (2%)
    pallas_call x1, Pallas kernels, body(): pl.pallas_call(finish_kernel, out_shape=jax.ShapeDtypeStruct((ROWS, FEATS...  53.7 us
    pallas_call x1, Pallas kernels, body(): pl.pallas_call(gather_kernel, out_shape=jax.ShapeDtypeStruct((n_ctx, ROWS...  27.6 us
    pallas_call x1, Pallas kernels, body(): pl.pallas_call(attention_kernel, out_shape=jax.ShapeDtypeStruct((REQS, SP...  6.07 us

profile of v2, /device:TPU:1, one launch (start us, length us, event | category | flops | bytes accessed | tf_op | source)
XLA Modules:
  0.0 89.2 jit_solution(1378988578926985632)
XLA Ops:
  0.0 27.6 %gather_queries.1 = bf16[64,16,384]{2,1,0:T(8,128)(2,1)} custom-call(bf16[16,384]{1,0:T(8,128)(2,1)} %q_ref.1), custom_call_target="tpu_custom_call" | custom-call | tf_op jit(solution)/shard_map/gather_queries/pallas_call | solution.py:513
  27.6 0.0 copy-start
  27.6 6.1 %attention.1.part_ref = bf16[4,256,512]{2,1,0:T(8,128)(2,1)} custom-call(s32[4,16]{1,0:T(4,128)} %table_ref.1, s32[4]{0:T(128)} %len_ref.1, bf16[1024,384]{1,0:T(8,128)(2,1)} %bitcast.2, bf16[2,512,384]{2,1,0:T(8,128)(2,1)} %k_ref.1, bf16[2,512,384]{2,1,0:T(8,128)(2,1)} %v_ref.1), custom_call_target="tpu_custom_call" | custom-call | tf_op jit(solution)/shard_map/attention/pallas_call | solution.py:522
  33.7 0.0 copy-done
  33.7 0.6 reshape.7.gain_ref
  34.2 53.7 %merge_project_norm.1 = bf16[16,384]{1,0:T(8,128)(2,1)} custom-call(bf16[4,256,512]{2,1,0:T(8,128)(2,1)} %attention.1.part_ref, bf16[48,384]{1,0:T(8,128)(2,1)} %bitcast.3, f32[1,384]{1,0:T(1,128)} %reshape.7.gain_ref), custom_call_target="tpu_custom_call" | custom-call | tf_op jit(solution)/shard_map/merge_project_norm/pallas_call | solution.py:529
  87.9 1.3 %copy.9 = bf16[16,384]{1,0:T(8,128)(2,1)} copy(bf16[16,384]{1,0:T(8,128)(2,1)} %merge_project_norm.1) | data formatting | bytes 24576
Async XLA Ops:
  27.6 6.1 %copy-start = (f32[384]{0:T(512)S(1)}, f32[384]{0:T(512)}, u32[]{:S(2)}) copy-start(f32[384]{0:T(512)} %param.13) | copy-start | bytes 4612

commit v3 on v2

--- a/solution.py
+++ b/solution.py
@@ -37,10 +37,9 @@
     pl.semaphore_signal(sem, inc=1, device_id=device, device_id_type=pl.DeviceIdType.MESH)
 
 
-def gather_kernel(q_ref, out_ref, own_sem, send_plane, send_near, send_far, recv):
+def gather_kernel(q_ref, out_ref, own_sem, send_plane, send_x, recv):
     me = lax.axis_index("ctx")
     x, j = me // PLANE, me % PLANE
-    up, down = (x + 1) % REQS, (x + REQS - 1) % REQS
     barrier = pltpu.get_barrier_semaphore()
 
     def greet(k, c):
@@ -48,87 +47,58 @@
         return c
 
     lax.fori_loop(1, PLANE, greet, 0)
-    for there in (up, down):
-        signal(barrier, {"ctx": there * PLANE + j})
+    for dx in range(1, REQS):
+        signal(barrier, {"ctx": (x + dx) % REQS * PLANE + j})
     own = pltpu.make_async_copy(q_ref, out_ref.at[me], own_sem)
     own.start()
-    pl.semaphore_wait(barrier, PLANE - 1 + 2)
-
-    def block_of(plane, k):
-        return plane * PLANE + (j + PLANE - k) % PLANE
+    pl.semaphore_wait(barrier, PLANE - 1 + REQS - 1)
 
     def to_plane(k):
         there = x * PLANE + (j + k) % PLANE
         return remote(q_ref, out_ref.at[me], send_plane.at[k], recv.at[me], {"ctx": there})
 
-    def pass_on(plane, there, k, sem):
-        block = block_of(plane, k)
-        src = q_ref if isinstance(k, int) and k == 0 and plane is x else out_ref.at[block]
-        return remote(src, out_ref.at[block], sem, recv.at[block], {"ctx": there * PLANE + j})
-
-    def near(k):
-        return [pass_on(x, up, k, send_near.at[0, k]), pass_on(x, down, k, send_near.at[1, k])]
-
-    def far(i):
-        return [
-            pass_on(down, up, 2 * i, send_far.at[2 * i]),
-            pass_on(up, down, 2 * i + 1, send_far.at[2 * i + 1]),
-        ]
-
-    def arrived(plane, k):
-        block = block_of(plane, k)
-        pltpu.make_async_copy(out_ref.at[block], out_ref.at[block], recv.at[block]).wait()
+    def to_x(k, dx):
+        block = x * PLANE + (j + PLANE - k) % PLANE
+        there = (x + dx) % REQS * PLANE + j
+        src = q_ref if isinstance(k, int) and k == 0 else out_ref.at[block]
+        return remote(
+            src, out_ref.at[block], send_x.at[dx - 1, k], recv.at[block], {"ctx": there}
+        )
 
     def start_plane(k, c):
         to_plane(k).start()
         return c
 
-    for copy in near(0):
-        copy.start()
+    for dx in range(1, REQS):
+        to_x(0, dx).start()
     lax.fori_loop(1, PLANE, start_plane, 0)
 
-    def forward(k):
-        arrived(x, k)
-        for copy in near(k):
-            copy.start()
-
-    def relay(i):
-        arrived(down, 2 * i)
-        far(i)[0].start()
-        arrived(up, 2 * i + 1)
-        far(i)[1].start()
-
-    forward(1)
-
-    def step(i, c):
-        forward(2 * i)
-        forward(2 * i + 1)
-        relay(i - 1)
-        return c
-
-    lax.fori_loop(1, PLANE // 2, step, 0)
-    relay(PLANE // 2 - 1)
-
-    def rest(i, c):
-        arrived(down, 2 * i + 1)
-        arrived(up, 2 * i)
-        arrived((x + 2) % REQS, 2 * i)
-        arrived((x + 2) % REQS, 2 * i + 1)
-        for copy in far(i):
-            copy.wait_send()
-        return c
-
-    lax.fori_loop(0, PLANE // 2, rest, 0)
+    def forward(k, c):
+        block = x * PLANE + (j + PLANE - k) % PLANE
+        pltpu.make_async_copy(out_ref.at[block], out_ref.at[block], recv.at[block]).wait()
+        for dx in range(1, REQS):
+            to_x(k, dx).start()
+        return c
+
+    lax.fori_loop(1, PLANE, forward, 0)
+
+    def arrive(k, c):
+        for dx in range(1, REQS):
+            block = (x + dx) % REQS * PLANE + (j + PLANE - k) % PLANE
+            pltpu.make_async_copy(out_ref.at[block], out_ref.at[block], recv.at[block]).wait()
+        return c
+
+    lax.fori_loop(0, PLANE, arrive, 0)
 
     def sent(k, c):
         to_plane(k).wait_send()
-        for copy in near(k):
-            copy.wait_send()
+        for dx in range(1, REQS):
+            to_x(k, dx).wait_send()
         return c
 
     lax.fori_loop(1, PLANE, sent, 0)
-    for copy in near(0):
-        copy.wait_send()
+    for dx in range(1, REQS):
+        to_x(0, dx).wait_send()
     own.wait()
 
 
@@ -515,7 +485,7 @@
         out_shape=jax.ShapeDtypeStruct((n_ctx, ROWS, FEATS), bf16),
         in_specs=[vmem],
         out_specs=vmem,
-        scratch_shapes=[dma, dma((PLANE,)), dma((2, PLANE)), dma((PLANE,)), dma((n_ctx,))],
+        scratch_shapes=[dma, dma((PLANE,)), dma((REQS - 1, PLANE)), dma((n_ctx,))],
         compiler_params=pltpu.CompilerParams(collective_id=0, has_side_effects=True),
         name="gather_queries",
     )(queries)

time: 89.5 us -> 83.9 us (0.937)
  Pallas kernels: 87.3 us -> 81.7 us
    pallas_call x1, Pallas kernels: 27.6 us -> 23 us  [body(): pl.pallas_call(gather_kernel, out_shape=jax.ShapeDtypeStruct((n_ctx, ROWS...]
where the time goes in v3:
time: 83.9 us; the launch traced here: 83.6 us
  Pallas kernels  81.7 us (97%)
  local copies, waits for them, and re-layouts  1.88 us (2%)
    pallas_call x1, Pallas kernels, body(): pl.pallas_call(finish_kernel, out_shape=jax.ShapeDtypeStruct((ROWS, FEATS...  53.1 us
    pallas_call x1, Pallas kernels, body(): pl.pallas_call(gather_kernel, out_shape=jax.ShapeDtypeStruct((n_ctx, ROWS...  23 us
    pallas_call x1, Pallas kernels, body(): pl.pallas_call(attention_kernel, out_shape=jax.ShapeDtypeStruct((REQS, SP...  5.57 us

profile of v3, /device:TPU:1, one launch (start us, length us, event | category | flops | bytes accessed | tf_op | source)
XLA Modules:
  0.0 83.6 jit_solution(14473540584100993449)
XLA Ops:
  0.0 23.0 %gather_queries.1 = bf16[64,16,384]{2,1,0:T(8,128)(2,1)} custom-call(bf16[16,384]{1,0:T(8,128)(2,1)} %q_ref.1), custom_call_target="tpu_custom_call" | custom-call | tf_op jit(solution)/shard_map/gather_queries/pallas_call | solution.py:483
  23.0 0.0 copy-start
  23.0 5.6 %attention.1.part_ref = bf16[4,256,512]{2,1,0:T(8,128)(2,1)} custom-call(s32[4,16]{1,0:T(4,128)} %table_ref.1, s32[4]{0:T(128)} %len_ref.1, bf16[1024,384]{1,0:T(8,128)(2,1)} %bitcast.2, bf16[2,512,384]{2,1,0:T(8,128)(2,1)} %k_ref.1, bf16[2,512,384]{2,1,0:T(8,128)(2,1)} %v_ref.1), custom_call_target="tpu_custom_call" | custom-call | tf_op jit(solution)/shard_map/attention/pallas_call | solution.py:492
  28.6 0.0 copy-done
  28.6 0.6 reshape.7.gain_ref
  29.2 53.1 %merge_project_norm.1 = bf16[16,384]{1,0:T(8,128)(2,1)} custom-call(bf16[4,256,512]{2,1,0:T(8,128)(2,1)} %attention.1.part_ref, bf16[48,384]{1,0:T(8,128)(2,1)} %bitcast.3, f32[1,384]{1,0:T(1,128)} %reshape.7.gain_ref), custom_call_target="tpu_custom_call" | custom-call | tf_op jit(solution)/shard_map/merge_project_norm/pallas_call | solution.py:499
  82.3 1.3 %copy.9 = bf16[16,384]{1,0:T(8,128)(2,1)} copy(bf16[16,384]{1,0:T(8,128)(2,1)} %merge_project_norm.1) | data formatting | bytes 24576
Async XLA Ops:
  23.0 5.6 %copy-start = (f32[384]{0:T(512)S(1)}, f32[384]{0:T(512)}, u32[]{:S(2)}) copy-start(f32[384]{0:T(512)} %param.13) | copy-start | bytes 4612

commit v4 on v3

--- a/solution.py
+++ b/solution.py
@@ -113,93 +113,80 @@
     return jnp.where(lane < 4 * HEADS_DEV, picked, 0.0).astype(jnp.bfloat16)
 
 
-def attention_kernel(table_ref, len_ref, q_ref, k_ref, v_ref, out_ref):
-    slots = k_ref.shape[0]
+def attend(slot_id, s, table_ref, len_ref, q_ref, k_ref, v_ref):
     block_rows = k_ref.shape[1]
-    me = lax.axis_index("ctx")
     scale = 1.0 / math.sqrt(HD)
-    empty_parts = split_parts(jnp.full((SPAN, 128), NEG, jnp.float32))
+    request = jnp.int32(-1)
+    reach = jnp.int32(-(1 << 28))
     for r in range(REQS):
-        out_ref[r, :, :FEATS] = jnp.zeros((SPAN, FEATS), jnp.bfloat16)
-        out_ref[r, :, FEATS:] = empty_parts
-    before = None
-    for s in range(slots):
-        slot_id = me * slots + s
-        found = jnp.int32(-1)
+        for b in range(table_ref.shape[1]):
+            hit = table_ref[r, b] == slot_id
+            request = jnp.where(hit, r, request)
+            reach = jnp.where(hit, len_ref[r] - b * block_rows, reach)
+    diff = (
+        lax.broadcasted_iota(jnp.int32, (SPAN, block_rows), 1)
+        - lax.broadcasted_iota(jnp.int32, (SPAN, block_rows), 0)
+    )
+    visible = diff <= reach
+    query = q_ref[:SPAN, :]
+    for r in range(1, REQS):
+        query = jnp.where(request == r, q_ref[r * SPAN : (r + 1) * SPAN, :], query)
+    tiles = [jnp.zeros((SPAN, 128), jnp.float32) for _ in range(FEATS // 128)]
+    lane = lax.broadcasted_iota(jnp.int32, (SPAN, 128), 1)
+    lse = jnp.full((SPAN, 128), NEG, jnp.float32)
+    for h in range(HEADS_DEV):
+        first, last = h * HD // 128, (h * HD + HD + 127) // 128
+        lo, hi = first * 128, last * 128
+        col = lo + lax.broadcasted_iota(jnp.int32, (SPAN, hi - lo), 1)
+        mine = (col >= h * HD) & (col < h * HD + HD)
+        part = query[:, lo:hi]
+        part = jnp.where(mine, part, jnp.zeros_like(part))
+        scores = lax.dot_general(
+            part, k_ref[s, :, lo:hi], (((1,), (1,)), ((), ())),
+            preferred_element_type=jnp.float32,
+        ) * scale
+        scores = jnp.where(visible, scores, NEG)
+        top = jnp.max(scores, axis=1, keepdims=True)
+        weights = jnp.where(visible, jnp.exp(scores - top), 0.0)
+        total = jnp.sum(weights, axis=1, keepdims=True)
+        mixed = jnp.dot(
+            weights.astype(jnp.bfloat16), v_ref[s, :, lo:hi],
+            preferred_element_type=jnp.float32,
+        )
+        some = total > 0.0
+        safe = jnp.where(some, total, 1.0)
+        mixed = jnp.where(mine, mixed * (1.0 / safe), 0.0)
+        for t in range(first, last):
+            tiles[t] = tiles[t] + mixed[:, t * 128 - lo : t * 128 - lo + 128]
+        level = jnp.where(some, top + jnp.log(safe), NEG)
+        lse = jnp.where(lane // 4 == h, level, lse)
+    return request, tiles, lse
+
+
+def merge_slots(one, two, part_ref):
+    lane = lax.broadcasted_iota(jnp.int32, (SPAN, 128), 1)
+    held = jnp.where(one[0] == two[0], one[2], NEG)
+    best = jnp.maximum(held, two[2])
+    keep, take = jnp.exp(held - best), jnp.exp(two[2] - best)
+    mass = keep + take
+    keep, take = keep / mass, take / mass
+    level = best + jnp.log(mass)
+    for t in range(FEATS // 128):
+        col = t * 128 + lane
+        k_b = jnp.zeros((SPAN, 128), jnp.float32)
+        t_b = jnp.zeros((SPAN, 128), jnp.float32)
+        for h in range(HEADS_DEV):
+            if h * HD < t * 128 + 128 and h * HD + HD > t * 128:
+                mine = (col >= h * HD) & (col < h * HD + HD)
+                k_b = jnp.where(mine, keep[:, 4 * h : 4 * h + 1], k_b)
+                t_b = jnp.where(mine, take[:, 4 * h : 4 * h + 1], t_b)
+        merged = one[1][t] * k_b + two[1][t] * t_b
         for r in range(REQS):
-            for b in range(table_ref.shape[1]):
-                found = jnp.where(table_ref[r, b] == slot_id, r * 16 + b, found)
-        used = found >= 0
-        request = jnp.where(used, found // 16, 0)
-        first_key = jnp.where(used, found % 16 * block_rows, 1 << 28)
-        diff = (
-            lax.broadcasted_iota(jnp.int32, (SPAN, block_rows), 1)
-            - lax.broadcasted_iota(jnp.int32, (SPAN, block_rows), 0)
-        )
-        visible = diff <= len_ref[request] - first_key
-        query = q_ref[pl.ds(pl.multiple_of(request * SPAN, SPAN), SPAN), :]
-        tiles = [jnp.zeros((SPAN, 128), jnp.float32) for _ in range(FEATS // 128)]
-        lane = lax.broadcasted_iota(jnp.int32, (SPAN, 128), 1)
-        lse = jnp.full((SPAN, 128), NEG, jnp.float32)
-        for h in range(HEADS_DEV):
-            first, last = h * HD // 128, (h * HD + HD + 127) // 128
-            lo, hi = first * 128, last * 128
-            col = lo + lax.broadcasted_iota(jnp.int32, (SPAN, hi - lo), 1)
-            mine = (col >= h * HD) & (col < h * HD + HD)
-            part = query[:, lo:hi]
-            part = jnp.where(mine, part, jnp.zeros_like(part))
-            scores = lax.dot_general(
-                part, k_ref[s, :, lo:hi], (((1,), (1,)), ((), ())),
-                preferred_element_type=jnp.float32,
-            ) * scale
-            scores = jnp.where(visible, scores, NEG)
-            top = jnp.max(scores, axis=1, keepdims=True)
-            weights = jnp.where(visible, jnp.exp(scores - top), 0.0)
-            total = jnp.sum(weights, axis=1, keepdims=True)
-            mixed = jnp.dot(
-                weights.astype(jnp.bfloat16), v_ref[s, :, lo:hi],
-                preferred_element_type=jnp.float32,
-            )
-            some = total > 0.0
-            safe = jnp.where(some, total, 1.0)
-            mixed = jnp.where(mine, mixed * (1.0 / safe), 0.0)
-            for t in range(first, last):
-                tiles[t] = tiles[t] + mixed[:, t * 128 - lo : t * 128 - lo + 128]
-            level = jnp.where(some, top + jnp.log(safe), NEG)
-            lse = jnp.where(lane // 4 == h, level, lse)
-        if before is None:
-            before = (used, request)
-
-            @pl.when(used)
-            def _():
-                for t in range(FEATS // 128):
-                    out_ref[request, :, t * 128 : t * 128 + 128] = tiles[t].astype(jnp.bfloat16)
-                out_ref[request, :, FEATS:] = split_parts(lse)
-
-            first_tiles, first_lse = tiles, lse
-        else:
-            same = before[0] & used & (before[1] == request)
-            held = jnp.where(same, first_lse, NEG)
-            best = jnp.maximum(held, lse)
-            keep, take = jnp.exp(held - best), jnp.exp(lse - best)
-            mass = keep + take
-            keep, take = keep / mass, take / mass
-            level = best + jnp.log(mass)
-
-            @pl.when(used)
-            def _():
-                for t in range(FEATS // 128):
-                    col = t * 128 + lane
-                    k_b = jnp.zeros((SPAN, 128), jnp.float32)
-                    t_b = jnp.zeros((SPAN, 128), jnp.float32)
-                    for h in range(HEADS_DEV):
-                        if h * HD < t * 128 + 128 and h * HD + HD > t * 128:
-                            mine = (col >= h * HD) & (col < h * HD + HD)
-                            k_b = jnp.where(mine, keep[:, 4 * h : 4 * h + 1], k_b)
-                            t_b = jnp.where(mine, take[:, 4 * h : 4 * h + 1], t_b)
-                    merged = first_tiles[t] * k_b + tiles[t] * t_b
-                    out_ref[request, :, t * 128 : t * 128 + 128] = merged.astype(jnp.bfloat16)
-                out_ref[request, :, FEATS:] = split_parts(level)
+            picked = jnp.where(two[0] == r, merged, jnp.where(one[0] == r, one[1][t], 0.0))
+            part_ref[r, :, t * 128 : t * 128 + 128] = picked.astype(jnp.bfloat16)
+    for r in range(REQS):
+        picked = jnp.where(two[0] == r, level, jnp.where(one[0] == r, one[2], NEG))
+        part_ref[r, :, FEATS:] = split_parts(picked)
 
 
 def spread(columns, width):
@@ -210,8 +197,8 @@
 
 
 def finish_kernel(
-    part_ref, w_ref, gain_ref, out_ref,
-    relay_in, relay_out, recv_a, comb, recv_b, w_all, attn_own, attn_all, proj, recv_p, ssq_own, recv_s,
+    table_ref, len_ref, q_ref, k_ref, v_ref, w_ref, gain_ref, out_ref,
+    part_ref, relay_in, relay_out, recv_a, comb, recv_b, w_all, attn_own, attn_all, proj, recv_p, ssq_own, recv_s,
     sr_send, sr_recv, sa_send, sa_recv, sb_send, sb_recv, sw_send, sw_recv, sg_send, sg_recv,
     sp_send, sp_recv, ss_send, ss_recv, diag_sem,
 ):
@@ -239,7 +226,25 @@
     def _():
         signal(barrier, {"tensor": group, "ctx": tensor * YS + y})
 
+    slots = k_ref.shape[0]
+    one = attend(me * slots, 0, table_ref, len_ref, q_ref, k_ref, v_ref)
     pl.semaphore_wait(barrier, PLANE - 1 + 3 * (GROUPS - 1) + off_diag.astype(jnp.int32))
+
+    def to_y(k):
+        return remote(
+            w_ref, w_all.at[y], sw_send.at[k], sw_recv.at[k], {"ctx": group * YS + (y + k) % YS}
+        )
+
+    def start_y(k, c):
+        to_y(k).start()
+        return c
+
+    lax.fori_loop(1, YS, start_y, 0)
+    own_w = pltpu.make_async_copy(w_ref, w_all.at[y], diag_sem)
+    own_w.start()
+
+    two = attend(me * slots + 1, 1, table_ref, len_ref, q_ref, k_ref, v_ref)
+    merge_slots(one, two, part_ref)
 
     half = PLANE // 2
     toward = ((x + 1) % REQS, (x + REQS - 1) % REQS)
@@ -273,19 +278,6 @@
 
     lax.fori_loop(0, half, start_relays, 0)
     lax.fori_loop(0, half, start_near, 0)
-
-    def to_y(k):
-        return remote(
-            w_ref, w_all.at[y], sw_send.at[k], sw_recv.at[k], {"ctx": group * YS + (y + k) % YS}
-        )
-
-    def start_y(k, c):
-        to_y(k).start()
-        return c
-
-    lax.fori_loop(1, YS, start_y, 0)
-    own_w = pltpu.make_async_copy(w_ref, w_all.at[y], diag_sem)
-    own_w.start()
 
     to_heads = spread(FEATS, HD)
     to_lanes = spread(128, 4)
@@ -489,19 +481,13 @@
         compiler_params=pltpu.CompilerParams(collective_id=0, has_side_effects=True),
         name="gather_queries",
     )(queries)
-    parts = pl.pallas_call(
-        attention_kernel,
-        out_shape=jax.ShapeDtypeStruct((REQS, SPAN, WIDE), bf16),
-        in_specs=[smem, smem, vmem, vmem, vmem],
-        out_specs=vmem,
-        name="attention",
-    )(block_slot, cached_len, gathered.reshape(n_ctx * ROWS, FEATS), key_cache, value_cache)
     return pl.pallas_call(
         finish_kernel,
         out_shape=jax.ShapeDtypeStruct((ROWS, FEATS), bf16),
-        in_specs=[vmem] * 3,
+        in_specs=[smem] * 2 + [vmem] * 5,
         out_specs=vmem,
         scratch_shapes=[
+            pltpu.VMEM((REQS, SPAN, WIDE), bf16),
             pltpu.VMEM((2, PLANE // 2, ROWS, WIDE), bf16),
             pltpu.VMEM((2, PLANE // 2, ROWS, WIDE), bf16),
             pltpu.VMEM((2, PLANE, ROWS, WIDE), bf16),
@@ -524,8 +510,11 @@
             dma,
         ],
         compiler_params=pltpu.CompilerParams(collective_id=1, has_side_effects=True),
-        name="merge_project_norm",
-    )(parts, weight_rows, norm_gain.reshape(1, FEATS))
+        name="attend_merge_project_norm",
+    )(
+        block_slot, cached_len, gathered.reshape(n_ctx * ROWS, FEATS), key_cache, value_cache,
+        weight_rows, norm_gain.reshape(1, FEATS),
+    )
 
 
 def solution(mesh):

time: 83.9 us -> 81.2 us (0.968)
  Pallas kernels: 81.7 us -> 78.3 us
    pallas_call x1 -> x0, Pallas kernels: 5.57 us -> none  [body(): pl.pallas_call(attention_kernel, out_shape=jax.ShapeDtypeStruct((REQS, SP...]
    pallas_call x1, Pallas kernels: 53.1 us -> 55.3 us  [body(): pl.pallas_call(finish_kernel, out_shape=jax.ShapeDtypeStruct((ROWS, FEATS...]
where the time goes in v4:
time: 81.2 us; the launch traced here: 80.9 us
  Pallas kernels  78.3 us (96%)
  local copies, waits for them, and re-layouts  2.55 us (3%)
    pallas_call x1, Pallas kernels, body(): pl.pallas_call(finish_kernel, out_shape=jax.ShapeDtypeStruct((ROWS, FEATS...  55.3 us
    pallas_call x1, Pallas kernels, body(): pl.pallas_call(gather_kernel, out_shape=jax.ShapeDtypeStruct((n_ctx, ROWS...  23 us

profile of v4, /device:TPU:1, one launch (start us, length us, event | category | flops | bytes accessed | tf_op | source)
XLA Modules:
  0.0 80.9 jit_solution(10391841309029905340)
XLA Ops:
  0.0 1.2 %reshape.7.gain_ref = f32[1,384]{1,0:T(1,128)} reshape(f32[384]{0:T(512)} %param.13) | data formatting | bytes 3072 | tf_op jit(solution)/shard_map/reshape | solution.py:516
  1.2 23.0 %gather_queries.1 = bf16[64,16,384]{2,1,0:T(8,128)(2,1)} custom-call(bf16[16,384]{1,0:T(8,128)(2,1)} %q_ref.1), custom_call_target="tpu_custom_call" | custom-call | tf_op jit(solution)/shard_map/gather_queries/pallas_call | solution.py:475
  24.2 55.3 %attend_merge_project_norm.1 = bf16[16,384]{1,0:T(8,128)(2,1)} custom-call(s32[4,16]{1,0:T(4,128)} %table_ref.1, s32[4]{0:T(128)} %len_ref.1, bf16[1024,384]{1,0:T(8,128)(2,1)} %bitcast.2, bf16[2,512,384]{2,1,0:T(8,128)(2,1)} %k_ref.1, bf16[2,512,384]{2,1,0:T(8,128)(2,1)} %v_ref.1, bf16[48,384]{1,0:T(8,128)(2,1)} %bitcast.3, f32[1,384]{1,0:T(1,128)} %reshape.7.gain_ref), custom_call_target="tpu_custom_call" | custom-call | tf_op jit(solution)/shard_map/attend_merge_project_norm/pallas_call | solution.py:484
  79.5 1.3 %copy.9 = bf16[16,384]{1,0:T(8,128)(2,1)} copy(bf16[16,384]{1,0:T(8,128)(2,1)} %attend_merge_project_norm.1) | data formatting | bytes 24576

commit v5 on v4

--- a/solution.py
+++ b/solution.py
@@ -198,8 +198,8 @@
 
 def finish_kernel(
     table_ref, len_ref, q_ref, k_ref, v_ref, w_ref, gain_ref, out_ref,
-    part_ref, relay_in, relay_out, recv_a, comb, recv_b, w_all, attn_own, attn_all, proj, recv_p, ssq_own, recv_s,
-    sr_send, sr_recv, sa_send, sa_recv, sb_send, sb_recv, sw_send, sw_recv, sg_send, sg_recv,
+    part_ref, recv_a, comb, recv_b, w_all, attn_own, attn_all, proj, recv_p, ssq_own, recv_s,
+    sa_send, sa_recv, sb_send, sb_recv, sw_send, sw_recv, sg_send, sg_recv,
     sp_send, sp_recv, ss_send, ss_recv, diag_sem,
 ):
     me = lax.axis_index("ctx")
@@ -247,37 +247,25 @@
     merge_slots(one, two, part_ref)
 
     half = PLANE // 2
-    toward = ((x + 1) % REQS, (x + REQS - 1) % REQS)
 
     def rows_of(k):
         return pl.ds(pl.multiple_of((j + k) % PLANE * ROWS, ROWS), ROWS)
 
-    def to_relay(way, i):
-        return remote(
-            part_ref.at[(x + 2) % REQS, rows_of(2 * i + way)], relay_in.at[way, i],
-            sr_send.at[way, i], sr_recv.at[way, i], {"ctx": toward[way] * PLANE + j},
-        )
-
-    def to_near(way, i, relayed):
-        k = 2 * i + (way if relayed else 1 - way)
-        src = relay_out.at[way, i] if relayed else part_ref.at[toward[way], rows_of(k)]
-        return remote(
-            src, recv_a.at[way, k], sa_send.at[way, k], sa_recv.at[way, k],
-            {"ctx": toward[way] * PLANE + j},
-        )
-
-    def start_relays(t, c):
-        for way in range(2):
-            to_relay(way, (t + 1) % half).start()
-        return c
-
-    def start_near(t, c):
-        for way in range(2):
-            to_near(way, (t + 1) % half, False).start()
-        return c
-
-    lax.fori_loop(0, half, start_relays, 0)
-    lax.fori_loop(0, half, start_near, 0)
+    def to_x(dx, k):
+        there = (x + dx) % REQS
+        return remote(
+            part_ref.at[there, rows_of(k)], recv_a.at[dx - 1, k],
+            sa_send.at[dx - 1, k], sa_recv.at[dx - 1, k], {"ctx": there * PLANE + j},
+        )
+
+    def start_x(t, c):
+        i = (t + 1) % half
+        for k in (2 * i, 2 * i + 1):
+            for dx in (2, 1, 3):
+                to_x(dx, k).start()
+        return c
+
+    lax.fori_loop(0, half, start_x, 0)
 
     to_heads = spread(FEATS, HD)
     to_lanes = spread(128, 4)
@@ -301,29 +289,12 @@
         level = top + jnp.log(sum(jnp.exp(n - top) for n in narrow))
         return (mixed / mass).astype(jnp.bfloat16), split_parts(level)
 
-    def relay(t, c):
-        i = (t + 1) % half
-        for way in range(2):
-            to_relay(way, i).wait_recv()
-        merged = [
-            combine([relay_in[way, i], part_ref[toward[way], rows_of(2 * i + way), :]])
-            for way in range(2)
-        ]
-        for way in range(2):
-            relay_out[way, i, :, :FEATS] = merged[way][0]
-            relay_out[way, i, :, FEATS:] = merged[way][1]
-        for way in range(2):
-            to_near(way, i, True).start()
-        return c
-
-    lax.fori_loop(0, half, relay, 0)
-
     def owned(i):
-        for way in range(2):
-            to_near(way, i, False).wait_recv()
-            to_near(way, i, True).wait_recv()
+        for k in (2 * i, 2 * i + 1):
+            for dx in range(1, REQS):
+                to_x(dx, k).wait_recv()
         return [
-            combine([part_ref[x, rows_of(k), :], recv_a[0, k], recv_a[1, k]])
+            combine([part_ref[x, rows_of(k), :]] + [recv_a[at, k] for at in range(REQS - 1)])
             for k in (2 * i, 2 * i + 1)
         ]
 
@@ -437,14 +408,12 @@
     inverse = lax.rsqrt(total * (1.0 / D) + 1e-05)
     out_ref[...] = (summed * inverse * gain_ref[...]).astype(jnp.bfloat16)
 
-    def sent_a(i, c):
-        for way in range(2):
-            to_relay(way, i).wait_send()
-            to_near(way, i, False).wait_send()
-            to_near(way, i, True).wait_send()
-        return c
-
-    lax.fori_loop(0, half, sent_a, 0)
+    def sent_a(k, c):
+        for dx in range(1, REQS):
+            to_x(dx, k).wait_send()
+        return c
+
+    lax.fori_loop(0, PLANE, sent_a, 0)
 
     def sent_plane(k, c):
         to_plane(k).wait_send()
@@ -488,9 +457,7 @@
         out_specs=vmem,
         scratch_shapes=[
             pltpu.VMEM((REQS, SPAN, WIDE), bf16),
-            pltpu.VMEM((2, PLANE // 2, ROWS, WIDE), bf16),
-            pltpu.VMEM((2, PLANE // 2, ROWS, WIDE), bf16),
-            pltpu.VMEM((2, PLANE, ROWS, WIDE), bf16),
+            pltpu.VMEM((REQS - 1, PLANE, ROWS, WIDE), bf16),
             pltpu.VMEM((PLANE, ROWS, WIDE), bf16),
             pltpu.VMEM((PLANE, ROWS, WIDE), bf16),
             pltpu.VMEM((YS, FEATS // YS, FEATS), bf16),
@@ -500,8 +467,7 @@
             pltpu.VMEM((GROUPS, ROWS, FEATS), bf16),
             pltpu.VMEM((ROWS, 128), f32),
             pltpu.VMEM((GROUPS, ROWS, 128), f32),
-            dma((2, PLANE // 2)), dma((2, PLANE // 2)),
-            dma((2, PLANE)), dma((2, PLANE)),
+            dma((REQS - 1, PLANE)), dma((REQS - 1, PLANE)),
             dma((PLANE,)), dma((PLANE,)),
             dma((YS,)), dma((YS,)),
             dma((GROUPS,)), dma((GROUPS,)),

time: 81.2 us -> 80.2 us (0.988)
  Pallas kernels: 78.3 us -> 77.3 us
    pallas_call x1, Pallas kernels: 55.3 us -> 54.4 us  [body(): pl.pallas_call(finish_kernel, out_shape=jax.ShapeDtypeStruct((ROWS, FEATS...]
where the time goes in v5:
time: 80.2 us; the launch traced here: 79.9 us
  Pallas kernels  77.3 us (96%)
  local copies, waits for them, and re-layouts  2.55 us (3%)
    pallas_call x1, Pallas kernels, body(): pl.pallas_call(finish_kernel, out_shape=jax.ShapeDtypeStruct((ROWS, FEATS...  54.4 us
    pallas_call x1, Pallas kernels, body(): pl.pallas_call(gather_kernel, out_shape=jax.ShapeDtypeStruct((n_ctx, ROWS...  23 us

profile of v5, /device:TPU:1, one launch (start us, length us, event | category | flops | bytes accessed | tf_op | source)
XLA Modules:
  0.0 79.9 jit_solution(17301165297563208730)
XLA Ops:
  0.0 1.2 %reshape.7.gain_ref = f32[1,384]{1,0:T(1,128)} reshape(f32[384]{0:T(512)} %param.13) | data formatting | bytes 3072 | tf_op jit(solution)/shard_map/reshape | solution.py:482
  1.2 23.0 %gather_queries.1 = bf16[64,16,384]{2,1,0:T(8,128)(2,1)} custom-call(bf16[16,384]{1,0:T(8,128)(2,1)} %q_ref.1), custom_call_target="tpu_custom_call" | custom-call | tf_op jit(solution)/shard_map/gather_queries/pallas_call | solution.py:444
  24.2 54.4 %attend_merge_project_norm.1 = bf16[16,384]{1,0:T(8,128)(2,1)} custom-call(s32[4,16]{1,0:T(4,128)} %table_ref.1, s32[4]{0:T(128)} %len_ref.1, bf16[1024,384]{1,0:T(8,128)(2,1)} %bitcast.2, bf16[2,512,384]{2,1,0:T(8,128)(2,1)} %k_ref.1, bf16[2,512,384]{2,1,0:T(8,128)(2,1)} %v_ref.1, bf16[48,384]{1,0:T(8,128)(2,1)} %bitcast.3, f32[1,384]{1,0:T(1,128)} %reshape.7.gain_ref), custom_call_target="tpu_custom_call" | custom-call | tf_op jit(solution)/shard_map/attend_merge_project_norm/pallas_call | solution.py:453
  78.6 1.3 %copy.9 = bf16[16,384]{1,0:T(8,128)(2,1)} copy(bf16[16,384]{1,0:T(8,128)(2,1)} %attend_merge_project_norm.1) | data formatting | bytes 24576
